TPU v7x, 256 devices: a whole 4x4x8 slice. The times are simulated.
256 devices in a mesh: ctx: 32 (over z, x_lo, core), head: 8 (over x_hi, y).
Axes of the slice: x: 4 (x_hi: 2, x_lo: 2; x = x_hi * 2 + x_lo), y: 4, z: 8, core: 2. Of those that a mesh axis runs over, the one named last changes fastest.
Arguments:
- block_order: int32 [64], replicated, may hold values from 0 to 63, as said below
- queries: bfloat16 [12288, 4096], P('ctx', 'head'), may hold values from -12 to 12
- key_head_matrix: bfloat16 [12288, 1024], P('ctx', 'head'), may hold values from -6 to 6
- value_head_matrix: bfloat16 [12288, 1024], P('ctx', 'head'), may hold values from -6 to 6
- out_weight: bfloat16 [4096, 4096], P('head'), may hold values from -0.125 to 0.125
- filter_taps: float32 [128, 4096], P(None, 'head'), may hold values from -0.5 to 0.5
- skip_gain: float32 [4096], P('head'), may hold values from 0.5 to 1.5
- gate_values: bfloat16 [12288, 4096], P('ctx', 'head'), may hold values from -4 to 4
Outputs:
- mixed_out: bfloat16 [12288, 4096], P('ctx', 'head')
Inputs may be any that keep to these rules, and one draw needn't show every extreme that they name: A permutation of the 64 sequence blocks; for every d, block_order[2 d] < 32 and block_order[2 d] + block_order[2 d + 1] = 63.
All inputs are finite; a program needn't handle non-finite values.
Results may differ from a plain program's by a relative error of at most 0.015.
Values may be sent and summed in bfloat16 or wider, within the bound.
No kernel may reach another device: no remote copies, remote signals or barrier semaphores. Data moves between devices by JAX's collectives and lax.ppermute only.
A program may use at most 64 MiB of HBM per device.

v0:
```python
import math

import jax
import jax.numpy as jnp
from jax import lax
from jax.sharding import PartitionSpec as P

HEAD_WIDTH = 128
QUERY_PER_KV = 4


def side_by_side(arrays, axis, dim, along):
    widths = [a.shape[along] for a in arrays]
    both = jnp.concatenate(arrays, axis=along)
    out = lax.all_gather(both, axis, axis=dim, tiled=True)
    return tuple(jnp.split(out, [sum(widths[:k]) for k in range(1, len(widths))], axis=along))


def in_blocks(x, dim, size):
    shape = x.shape
    tiles = x.reshape(*shape[:dim], size, shape[dim] // size, *shape[dim + 1 :])
    return jnp.moveaxis(tiles, dim, 0)


def sum_at_owner(x, axis, dim):
    size = lax.axis_size(axis)
    tiles = lax.all_to_all(in_blocks(x, dim, size), axis, 0, 0, tiled=True)
    return jnp.sum(tiles.astype(jnp.float32), axis=0)


def lookup(table_values, index_values):
    matches = jnp.arange(table_values.shape[0], dtype=jnp.int32)[None, :] == index_values[:, None]
    return jnp.sum(jnp.where(matches, table_values[None, :], 0), axis=1)


def shards(
    block_order,
    queries,
    key_head_matrix,
    value_head_matrix,
    out_weight,
    filter_taps,
    skip_gain,
    gate_values,
):
    local_rows = queries.shape[0]
    block_rows = local_rows // 2
    shared_heads = key_head_matrix.shape[1] // HEAD_WIDTH
    position = lax.axis_index("ctx")
    own_blocks = 2 * position + jnp.arange(2, dtype=jnp.int32)
    own_order = lookup(block_order, own_blocks)
    query_place = (
        own_order[:, None] * block_rows + jnp.arange(block_rows, dtype=jnp.int32)[None, :]
    ).reshape(local_rows)
    query_heads = queries.reshape(local_rows, shared_heads, QUERY_PER_KV, HEAD_WIDTH)
    scaling = 1.0 / math.sqrt(HEAD_WIDTH)

    def attend_block(state_now, key_block, value_block, offset):
        running, row_total, summed = state_now
        key_count = key_block.shape[0]
        key_index = offset + jnp.arange(key_count, dtype=jnp.int32)
        key_place = (
            lookup(block_order, key_index // block_rows) * block_rows + key_index % block_rows
        )
        allowed = key_place[None, :] <= query_place[:, None]
        scores = (
            jnp.einsum("qhgd,khd->hgqk", query_heads, key_block, preferred_element_type=jnp.float32)
            * scaling
        )
        scores = jnp.where(allowed, scores, -1e30)
        newest = jnp.maximum(running, jnp.max(scores, axis=-1))
        weight = jnp.where(allowed, jnp.exp(scores - newest[..., None]), 0.0)
        factor = jnp.exp(running - newest)
        row_total = row_total * factor + jnp.sum(weight, axis=-1)
        summed = summed * factor[..., None] + jnp.einsum(
            "hgqk,khd->hgqd",
            weight.astype(jnp.bfloat16),
            value_block,
            preferred_element_type=jnp.float32,
        )
        return (newest, row_total, summed)

    start_state = (
        jnp.full((shared_heads, QUERY_PER_KV, local_rows), -1e30, jnp.float32),
        jnp.zeros((shared_heads, QUERY_PER_KV, local_rows), jnp.float32),
        jnp.zeros((shared_heads, QUERY_PER_KV, local_rows, HEAD_WIDTH), jnp.float32),
    )
    key_piece, value_piece = side_by_side((key_head_matrix, value_head_matrix), "ctx", 0, 1)
    key_count = key_piece.shape[0]
    sub_rows = math.gcd(key_count, 1024)
    steps_count = key_count // sub_rows
    key_split = key_piece.reshape(steps_count, sub_rows, shared_heads, HEAD_WIDTH)
    value_split = value_piece.reshape(steps_count, sub_rows, shared_heads, HEAD_WIDTH)

    def one_step(carried, operands):
        key_block, value_block, block_number = operands
        return (attend_block(carried, key_block, value_block, block_number * sub_rows), None)

    result, unused = lax.scan(
        one_step, start_state, (key_split, value_split, jnp.arange(steps_count, dtype=jnp.int32))
    )
    running, row_total, summed = result
    attended = (
        jnp.transpose(summed / row_total[..., None], (2, 0, 1, 3))
        .reshape(local_rows, -1)
        .astype(jnp.bfloat16)
    )
    partials = jnp.dot(attended, out_weight, preferred_element_type=jnp.float32)
    projected = sum_at_owner(partials.astype(jnp.bfloat16), "head", 1).astype(jnp.bfloat16)
    channels = projected.shape[1]
    reach_rows = filter_taps.shape[0] - 1
    blocks_here = projected.reshape(2, block_rows, channels)
    tail_rows = blocks_here[:, block_rows - reach_rows :, :]
    wanted = own_order - 1
    piece = lax.all_gather(tail_rows, "ctx", axis=0, tiled=True)
    piece_count = piece.shape[0]
    held_blocks = lookup(block_order, jnp.arange(piece_count, dtype=jnp.int32))
    matches = (held_blocks[None, :] == wanted[:, None]).astype(jnp.bfloat16)
    halo_rows = jnp.einsum(
        "sn,nrc->src", matches, piece, preferred_element_type=jnp.float32
    ).astype(jnp.bfloat16)
    extended = jnp.concatenate([halo_rows, blocks_here], axis=1).astype(jnp.float32)
    reversed_taps = jnp.flip(filter_taps, 0)
    kernel = reversed_taps[:, None, :]
    filtered = lax.conv_general_dilated(
        extended,
        kernel,
        (1,),
        "VALID",
        dimension_numbers=("NHC", "HIO", "NHC"),
        feature_group_count=channels,
        precision=lax.Precision.HIGHEST,
    )
    gate_here = gate_values.reshape(2, block_rows, channels).astype(jnp.float32)
    mixed_rows = gate_here * (filtered + skip_gain[None, None, :] * blocks_here.astype(jnp.float32))
    return mixed_rows.reshape(local_rows, channels).astype(jnp.bfloat16)


def solution(mesh):
    return jax.shard_map(
        shards,
        mesh=mesh,
        in_specs=(
            P(),
            P("ctx", "head"),
            P("ctx", "head"),
            P("ctx", "head"),
            P("head", None),
            P(None, "head"),
            P("head"),
            P("ctx", "head"),
        ),
        out_specs=P("ctx", "head"),
        check_vma=False,
    )
```

profile of v0, /device:TPU:1, one launch (start us, length us, event | category | flops | bytes accessed | tf_op | source)
XLA Modules:
  0.0 391.9 jit_solution(11266941806770182200)
XLA Ops:
  10.6 71.8 %all-gather.3.cloned.1.call-done = bf16[12288,256]{1,0:T(8,128)(2,1)} async-done(((bf16[384,256]{1,0:T(8,128)(2,1)}), bf16[12288,256]{1,0:T(8,128)(2,1)}) %all-gather.3.cloned.1.call-update) | async-done | bytes 6291472 | tf_op jit(solution)/shard_map/all_gather | solution.py:15
  87.2 156.6 %while.17 = (s32[]{:T(128)}, f32[1,4,384]{2,1,0:T(4,128)S(1)}, f32[1,4,384]{2,1,0:T(4,128)S(1)}, f32[1,4,384,128]{3,2,1,0:T(8,128)S(1)}, s32[12]{0:T(128)S(1)}, ...) while((s32[]{:T(128)}, f32[1,4,384]{2,1,0:T(4,128)S(1)}, ...), condition=%wide.region_6.7_spmd.clone, body=%wide.region_2.6_spmd.clone.sunk | while | flops 826960256 | bytes 48233928 | solution.py:99
  89.0 4.8 %fusion.66 = (f32[4,384]{1,0:T(4,128)S(1)}, f32[1024,384,4]{1,0,2:T(8,128)}) fusion(pred[384,1024]{0,1:T(8,128)(4,1)S(1)} %broadcast_compare_fusion.2, bf16[384,1,4,128]{3,0,2,1:T(8,128)(2,1)S(1)} %get-tuple-element.342, bf16[12,1024,1,128]{3,1,2,0:T(8,128)(2,1)} %get-tuple-element.341, s32[]{:T(128)} %get-tuple-element.322), kind=kOutput, calls=%fused_computation.3.clone.1 | convolution fusion | flops 407370240 | bytes 7346688 | tf_op jit(solution)/shard_map/while/body/eval_jaxpr/qhgd,khd->hgqk/dot_general | solution.py:67
  93.8 4.8 %fusion.69 = f32[1,4,384,128]{3,2,1,0:T(8,128)S(1)} fusion(f32[1024,384,4]{1,0,2:T(8,128)} %get-tuple-element.307, f32[4,384]{1,0:T(4,128)S(1)} %bitcast.111, pred[384,1024]{0,1:T(8,128)(4,1)S(1)} %broadcast_compare_fusion.2, f32[1,4,384,128]{3,2,1,0:T(8,128)S(1)} %get-tuple-element.325, f32[4,384]{1,0:T(4,128)S(1)} %get-tuple-element.308, ...), kind=kOutput, calls=%fused_computation.10.clone.1 | convolution fusion | flops 411107328 | bytes 8532481 | tf_op jit(solution)/shard_map/while/body/eval_jaxpr/hgqk,khd->hgqd/dot_general | solution.py:75
  106.9 4.8 %fusion.69 = f32[1,4,384,128]{3,2,1,0:T(8,128)S(1)} fusion(f32[1024,384,4]{1,0,2:T(8,128)} %get-tuple-element.307, f32[4,384]{1,0:T(4,128)S(1)} %bitcast.111, pred[384,1024]{0,1:T(8,128)(4,1)S(1)} %broadcast_compare_fusion.2, f32[1,4,384,128]{3,2,1,0:T(8,128)S(1)} %get-tuple-element.325, f32[4,384]{1,0:T(4,128)S(1)} %get-tuple-element.308, ...), kind=kOutput, calls=%fused_computation.10.clone.1 | convolution fusion | flops 411107328 | bytes 8532481 | tf_op jit(solution)/shard_map/while/body/eval_jaxpr/hgqk,khd->hgqd/dot_general | solution.py:75
  115.2 4.8 %fusion.66 = (f32[4,384]{1,0:T(4,128)S(1)}, f32[1024,384,4]{1,0,2:T(8,128)}) fusion(pred[384,1024]{0,1:T(8,128)(4,1)S(1)} %broadcast_compare_fusion.2, bf16[384,1,4,128]{3,0,2,1:T(8,128)(2,1)S(1)} %get-tuple-element.342, bf16[12,1024,1,128]{3,1,2,0:T(8,128)(2,1)} %get-tuple-element.341, s32[]{:T(128)} %get-tuple-element.322), kind=kOutput, calls=%fused_computation.3.clone.1 | convolution fusion | flops 407370240 | bytes 7346688 | tf_op jit(solution)/shard_map/while/body/eval_jaxpr/qhgd,khd->hgqk/dot_general | solution.py:67
  120.0 4.8 %fusion.69 = f32[1,4,384,128]{3,2,1,0:T(8,128)S(1)} fusion(f32[1024,384,4]{1,0,2:T(8,128)} %get-tuple-element.307, f32[4,384]{1,0:T(4,128)S(1)} %bitcast.111, pred[384,1024]{0,1:T(8,128)(4,1)S(1)} %broadcast_compare_fusion.2, f32[1,4,384,128]{3,2,1,0:T(8,128)S(1)} %get-tuple-element.325, f32[4,384]{1,0:T(4,128)S(1)} %get-tuple-element.308, ...), kind=kOutput, calls=%fused_computation.10.clone.1 | convolution fusion | flops 411107328 | bytes 8532481 | tf_op jit(solution)/shard_map/while/body/eval_jaxpr/hgqk,khd->hgqd/dot_general | solution.py:75
  128.2 4.8 %fusion.66 = (f32[4,384]{1,0:T(4,128)S(1)}, f32[1024,384,4]{1,0,2:T(8,128)}) fusion(pred[384,1024]{0,1:T(8,128)(4,1)S(1)} %broadcast_compare_fusion.2, bf16[384,1,4,128]{3,0,2,1:T(8,128)(2,1)S(1)} %get-tuple-element.342, bf16[12,1024,1,128]{3,1,2,0:T(8,128)(2,1)} %get-tuple-element.341, s32[]{:T(128)} %get-tuple-element.322), kind=kOutput, calls=%fused_computation.3.clone.1 | convolution fusion | flops 407370240 | bytes 7346688 | tf_op jit(solution)/shard_map/while/body/eval_jaxpr/qhgd,khd->hgqk/dot_general | solution.py:67
  133.0 4.8 %fusion.69 = f32[1,4,384,128]{3,2,1,0:T(8,128)S(1)} fusion(f32[1024,384,4]{1,0,2:T(8,128)} %get-tuple-element.307, f32[4,384]{1,0:T(4,128)S(1)} %bitcast.111, pred[384,1024]{0,1:T(8,128)(4,1)S(1)} %broadcast_compare_fusion.2, f32[1,4,384,128]{3,2,1,0:T(8,128)S(1)} %get-tuple-element.325, f32[4,384]{1,0:T(4,128)S(1)} %get-tuple-element.308, ...), kind=kOutput, calls=%fused_computation.10.clone.1 | convolution fusion | flops 411107328 | bytes 8532481 | tf_op jit(solution)/shard_map/while/body/eval_jaxpr/hgqk,khd->hgqd/dot_general | solution.py:75
  141.3 4.8 %fusion.66 = (f32[4,384]{1,0:T(4,128)S(1)}, f32[1024,384,4]{1,0,2:T(8,128)}) fusion(pred[384,1024]{0,1:T(8,128)(4,1)S(1)} %broadcast_compare_fusion.2, bf16[384,1,4,128]{3,0,2,1:T(8,128)(2,1)S(1)} %get-tuple-element.342, bf16[12,1024,1,128]{3,1,2,0:T(8,128)(2,1)} %get-tuple-element.341, s32[]{:T(128)} %get-tuple-element.322), kind=kOutput, calls=%fused_computation.3.clone.1 | convolution fusion | flops 407370240 | bytes 7346688 | tf_op jit(solution)/shard_map/while/body/eval_jaxpr/qhgd,khd->hgqk/dot_general | solution.py:67
  146.1 4.8 %fusion.69 = f32[1,4,384,128]{3,2,1,0:T(8,128)S(1)} fusion(f32[1024,384,4]{1,0,2:T(8,128)} %get-tuple-element.307, f32[4,384]{1,0:T(4,128)S(1)} %bitcast.111, pred[384,1024]{0,1:T(8,128)(4,1)S(1)} %broadcast_compare_fusion.2, f32[1,4,384,128]{3,2,1,0:T(8,128)S(1)} %get-tuple-element.325, f32[4,384]{1,0:T(4,128)S(1)} %get-tuple-element.308, ...), kind=kOutput, calls=%fused_computation.10.clone.1 | convolution fusion | flops 411107328 | bytes 8532481 | tf_op jit(solution)/shard_map/while/body/eval_jaxpr/hgqk,khd->hgqd/dot_general | solution.py:75
  154.3 4.8 %fusion.66 = (f32[4,384]{1,0:T(4,128)S(1)}, f32[1024,384,4]{1,0,2:T(8,128)}) fusion(pred[384,1024]{0,1:T(8,128)(4,1)S(1)} %broadcast_compare_fusion.2, bf16[384,1,4,128]{3,0,2,1:T(8,128)(2,1)S(1)} %get-tuple-element.342, bf16[12,1024,1,128]{3,1,2,0:T(8,128)(2,1)} %get-tuple-element.341, s32[]{:T(128)} %get-tuple-element.322), kind=kOutput, calls=%fused_computation.3.clone.1 | convolution fusion | flops 407370240 | bytes 7346688 | tf_op jit(solution)/shard_map/while/body/eval_jaxpr/qhgd,khd->hgqk/dot_general | solution.py:67
  159.1 4.8 %fusion.69 = f32[1,4,384,128]{3,2,1,0:T(8,128)S(1)} fusion(f32[1024,384,4]{1,0,2:T(8,128)} %get-tuple-element.307, f32[4,384]{1,0:T(4,128)S(1)} %bitcast.111, pred[384,1024]{0,1:T(8,128)(4,1)S(1)} %broadcast_compare_fusion.2, f32[1,4,384,128]{3,2,1,0:T(8,128)S(1)} %get-tuple-element.325, f32[4,384]{1,0:T(4,128)S(1)} %get-tuple-element.308, ...), kind=kOutput, calls=%fused_computation.10.clone.1 | convolution fusion | flops 411107328 | bytes 8532481 | tf_op jit(solution)/shard_map/while/body/eval_jaxpr/hgqk,khd->hgqd/dot_general | solution.py:75
  167.4 4.8 %fusion.66 = (f32[4,384]{1,0:T(4,128)S(1)}, f32[1024,384,4]{1,0,2:T(8,128)}) fusion(pred[384,1024]{0,1:T(8,128)(4,1)S(1)} %broadcast_compare_fusion.2, bf16[384,1,4,128]{3,0,2,1:T(8,128)(2,1)S(1)} %get-tuple-element.342, bf16[12,1024,1,128]{3,1,2,0:T(8,128)(2,1)} %get-tuple-element.341, s32[]{:T(128)} %get-tuple-element.322), kind=kOutput, calls=%fused_computation.3.clone.1 | convolution fusion | flops 407370240 | bytes 7346688 | tf_op jit(solution)/shard_map/while/body/eval_jaxpr/qhgd,khd->hgqk/dot_general | solution.py:67
  172.2 4.8 %fusion.69 = f32[1,4,384,128]{3,2,1,0:T(8,128)S(1)} fusion(f32[1024,384,4]{1,0,2:T(8,128)} %get-tuple-element.307, f32[4,384]{1,0:T(4,128)S(1)} %bitcast.111, pred[384,1024]{0,1:T(8,128)(4,1)S(1)} %broadcast_compare_fusion.2, f32[1,4,384,128]{3,2,1,0:T(8,128)S(1)} %get-tuple-element.325, f32[4,384]{1,0:T(4,128)S(1)} %get-tuple-element.308, ...), kind=kOutput, calls=%fused_computation.10.clone.1 | convolution fusion | flops 411107328 | bytes 8532481 | tf_op jit(solution)/shard_map/while/body/eval_jaxpr/hgqk,khd->hgqd/dot_general | solution.py:75
  185.2 4.8 %fusion.69 = f32[1,4,384,128]{3,2,1,0:T(8,128)S(1)} fusion(f32[1024,384,4]{1,0,2:T(8,128)} %get-tuple-element.307, f32[4,384]{1,0:T(4,128)S(1)} %bitcast.111, pred[384,1024]{0,1:T(8,128)(4,1)S(1)} %broadcast_compare_fusion.2, f32[1,4,384,128]{3,2,1,0:T(8,128)S(1)} %get-tuple-element.325, f32[4,384]{1,0:T(4,128)S(1)} %get-tuple-element.308, ...), kind=kOutput, calls=%fused_computation.10.clone.1 | convolution fusion | flops 411107328 | bytes 8532481 | tf_op jit(solution)/shard_map/while/body/eval_jaxpr/hgqk,khd->hgqd/dot_general | solution.py:75
  198.3 4.8 %fusion.69 = f32[1,4,384,128]{3,2,1,0:T(8,128)S(1)} fusion(f32[1024,384,4]{1,0,2:T(8,128)} %get-tuple-element.307, f32[4,384]{1,0:T(4,128)S(1)} %bitcast.111, pred[384,1024]{0,1:T(8,128)(4,1)S(1)} %broadcast_compare_fusion.2, f32[1,4,384,128]{3,2,1,0:T(8,128)S(1)} %get-tuple-element.325, f32[4,384]{1,0:T(4,128)S(1)} %get-tuple-element.308, ...), kind=kOutput, calls=%fused_computation.10.clone.1 | convolution fusion | flops 411107328 | bytes 8532481 | tf_op jit(solution)/shard_map/while/body/eval_jaxpr/hgqk,khd->hgqd/dot_general | solution.py:75
  211.3 4.8 %fusion.69 = f32[1,4,384,128]{3,2,1,0:T(8,128)S(1)} fusion(f32[1024,384,4]{1,0,2:T(8,128)} %get-tuple-element.307, f32[4,384]{1,0:T(4,128)S(1)} %bitcast.111, pred[384,1024]{0,1:T(8,128)(4,1)S(1)} %broadcast_compare_fusion.2, f32[1,4,384,128]{3,2,1,0:T(8,128)S(1)} %get-tuple-element.325, f32[4,384]{1,0:T(4,128)S(1)} %get-tuple-element.308, ...), kind=kOutput, calls=%fused_computation.10.clone.1 | convolution fusion | flops 411107328 | bytes 8532481 | tf_op jit(solution)/shard_map/while/body/eval_jaxpr/hgqk,khd->hgqd/dot_general | solution.py:75
  224.4 4.8 %fusion.69 = f32[1,4,384,128]{3,2,1,0:T(8,128)S(1)} fusion(f32[1024,384,4]{1,0,2:T(8,128)} %get-tuple-element.307, f32[4,384]{1,0:T(4,128)S(1)} %bitcast.111, pred[384,1024]{0,1:T(8,128)(4,1)S(1)} %broadcast_compare_fusion.2, f32[1,4,384,128]{3,2,1,0:T(8,128)S(1)} %get-tuple-element.325, f32[4,384]{1,0:T(4,128)S(1)} %get-tuple-element.308, ...), kind=kOutput, calls=%fused_computation.10.clone.1 | convolution fusion | flops 411107328 | bytes 8532481 | tf_op jit(solution)/shard_map/while/body/eval_jaxpr/hgqk,khd->hgqd/dot_general | solution.py:75
  237.4 4.8 %fusion.69 = f32[1,4,384,128]{3,2,1,0:T(8,128)S(1)} fusion(f32[1024,384,4]{1,0,2:T(8,128)} %get-tuple-element.307, f32[4,384]{1,0:T(4,128)S(1)} %bitcast.111, pred[384,1024]{0,1:T(8,128)(4,1)S(1)} %broadcast_compare_fusion.2, f32[1,4,384,128]{3,2,1,0:T(8,128)S(1)} %get-tuple-element.325, f32[4,384]{1,0:T(4,128)S(1)} %get-tuple-element.308, ...), kind=kOutput, calls=%fused_computation.10.clone.1 | convolution fusion | flops 411107328 | bytes 8532481 | tf_op jit(solution)/shard_map/while/body/eval_jaxpr/hgqk,khd->hgqd/dot_general | solution.py:75
  248.5 44.2 %all_to_all.5 = bf16[8,384,512]{2,1,0:T(8,128)(2,1)S(1)} all-to-all(bf16[8,384,512]{2,1,0:T(8,128)(2,1)S(1)} %bitcast.104), channel_id=1, replica_groups=mesh['ctx'=32,'head'=8] {'head'}, dimensions={0} | all-to-all | bytes 6291456 | tf_op jit(solution)/shard_map/all_to_all | solution.py:27
  296.5 67.8 %all-gather.5.cloned.1.call-done = bf16[64,127,512]{2,1,0:T(8,128)(2,1)} async-done(((bf16[2,127,512]{2,1,0:T(8,128)(2,1)}), bf16[64,127,512]{2,1,0:T(8,128)(2,1)}) %all-gather.5.cloned.1.call-update) | async-done | bytes 8323088 | tf_op jit(solution)/shard_map/all_gather | solution.py:115
  364.3 12.2 %fusion.35 = bf16[2,127,512]{2,0,1:T(2,128)(2,1)S(1)} fusion(bf16[64,127,512]{2,1,0:T(8,128)(2,1)} %all-gather.5.cloned.1.call-done, s32[64]{0:T(128)S(1)} %select_reduce_fusion.1, s32[2]{0:T(128)S(1)} %get-tuple-element.238), kind=kOutput, calls=%fused_computation.46 | convolution fusion | flops 16776320 | bytes 8583432 | tf_op jit(solution)/shard_map/sn,nrc->src/dot_general | solution.py:119
  376.5 7.5 %fusion.39 = f32[2,192,512]{2,0,1:T(2,128)S(1)} fusion(bf16[2,192,512]{2,0,1:T(2,128)(2,1)S(1)} %copy.49, bf16[2,127,512]{2,0,1:T(2,128)(2,1)S(1)} %fusion.35, f32[128,1,512]{2,0,1:T(8,128)S(1)} %bitcast.116), kind=kOutput, calls=%fused_computation.51 | convolution fusion | flops 303296512 | bytes 1701888 | tf_op jit(solution)/shard_map/conv_general_dilated | solution.py:125
  (193 shorter events, 79.6 us)
Async XLA Ops:
  6.5 75.9 %all-gather.3.cloned.1.call-start = ((), (), s32[]{:S(2)}) async-start(), calls=%async_computation.1 | async-start | bytes 6488064 | tf_op jit(solution)/shard_map/all_gather | solution.py:15
  8.2 356.1 %all-gather.5.cloned.1.call-start = ((), (), s32[]{:S(2)}) async-start(), calls=%async_computation.2 | async-start | bytes 8650752 | tf_op jit(solution)/shard_map/all_gather | solution.py:115
  10.6 76.6 %copy-start.2 = (s32[64]{0:T(128)S(1)}, s32[64]{0:T(128)}, u32[]{:S(2)}) copy-start(s32[64]{0:T(128)} %param.10) | copy-start | bytes 772
  93.8 4.8 %copy-start = (f32[1024,384,4]{1,0,2:T(8,128)S(1)}, f32[1024,384,4]{1,0,2:T(8,128)}, u32[]{:S(2)}) copy-start(f32[1024,384,4]{1,0,2:T(8,128)} %get-tuple-element.307) | copy-start | bytes 18874372 | tf_op jit(solution)/shard_map/while
  106.9 4.8 %copy-start = (f32[1024,384,4]{1,0,2:T(8,128)S(1)}, f32[1024,384,4]{1,0,2:T(8,128)}, u32[]{:S(2)}) copy-start(f32[1024,384,4]{1,0,2:T(8,128)} %get-tuple-element.307) | copy-start | bytes 18874372 | tf_op jit(solution)/shard_map/while
  119.9 4.8 %copy-start = (f32[1024,384,4]{1,0,2:T(8,128)S(1)}, f32[1024,384,4]{1,0,2:T(8,128)}, u32[]{:S(2)}) copy-start(f32[1024,384,4]{1,0,2:T(8,128)} %get-tuple-element.307) | copy-start | bytes 18874372 | tf_op jit(solution)/shard_map/while
  133.0 4.8 %copy-start = (f32[1024,384,4]{1,0,2:T(8,128)S(1)}, f32[1024,384,4]{1,0,2:T(8,128)}, u32[]{:S(2)}) copy-start(f32[1024,384,4]{1,0,2:T(8,128)} %get-tuple-element.307) | copy-start | bytes 18874372 | tf_op jit(solution)/shard_map/while
  146.0 4.8 %copy-start = (f32[1024,384,4]{1,0,2:T(8,128)S(1)}, f32[1024,384,4]{1,0,2:T(8,128)}, u32[]{:S(2)}) copy-start(f32[1024,384,4]{1,0,2:T(8,128)} %get-tuple-element.307) | copy-start | bytes 18874372 | tf_op jit(solution)/shard_map/while
  159.1 4.8 %copy-start = (f32[1024,384,4]{1,0,2:T(8,128)S(1)}, f32[1024,384,4]{1,0,2:T(8,128)}, u32[]{:S(2)}) copy-start(f32[1024,384,4]{1,0,2:T(8,128)} %get-tuple-element.307) | copy-start | bytes 18874372 | tf_op jit(solution)/shard_map/while
  172.2 4.8 %copy-start = (f32[1024,384,4]{1,0,2:T(8,128)S(1)}, f32[1024,384,4]{1,0,2:T(8,128)}, u32[]{:S(2)}) copy-start(f32[1024,384,4]{1,0,2:T(8,128)} %get-tuple-element.307) | copy-start | bytes 18874372 | tf_op jit(solution)/shard_map/while
  185.2 4.8 %copy-start = (f32[1024,384,4]{1,0,2:T(8,128)S(1)}, f32[1024,384,4]{1,0,2:T(8,128)}, u32[]{:S(2)}) copy-start(f32[1024,384,4]{1,0,2:T(8,128)} %get-tuple-element.307) | copy-start | bytes 18874372 | tf_op jit(solution)/shard_map/while
  198.3 4.8 %copy-start = (f32[1024,384,4]{1,0,2:T(8,128)S(1)}, f32[1024,384,4]{1,0,2:T(8,128)}, u32[]{:S(2)}) copy-start(f32[1024,384,4]{1,0,2:T(8,128)} %get-tuple-element.307) | copy-start | bytes 18874372 | tf_op jit(solution)/shard_map/while
  211.3 4.8 %copy-start = (f32[1024,384,4]{1,0,2:T(8,128)S(1)}, f32[1024,384,4]{1,0,2:T(8,128)}, u32[]{:S(2)}) copy-start(f32[1024,384,4]{1,0,2:T(8,128)} %get-tuple-element.307) | copy-start | bytes 18874372 | tf_op jit(solution)/shard_map/while
  224.4 4.8 %copy-start = (f32[1024,384,4]{1,0,2:T(8,128)S(1)}, f32[1024,384,4]{1,0,2:T(8,128)}, u32[]{:S(2)}) copy-start(f32[1024,384,4]{1,0,2:T(8,128)} %get-tuple-element.307) | copy-start | bytes 18874372 | tf_op jit(solution)/shard_map/while
  237.4 4.8 %copy-start = (f32[1024,384,4]{1,0,2:T(8,128)S(1)}, f32[1024,384,4]{1,0,2:T(8,128)}, u32[]{:S(2)}) copy-start(f32[1024,384,4]{1,0,2:T(8,128)} %get-tuple-element.307) | copy-start | bytes 18874372 | tf_op jit(solution)/shard_map/while
  376.5 7.5 %copy-start.1 = (bf16[384,512]{1,0:T(8,128)(2,1)S(1)}, bf16[384,512]{1,0:T(8,128)(2,1)}, u32[]{:S(2)}) copy-start(bf16[384,512]{1,0:T(8,128)(2,1)} %param.17) | copy-start | bytes 1179652
  376.5 7.5 %copy-start.3 = (f32[512]{0:T(512)S(1)}, f32[512]{0:T(512)}, u32[]{:S(2)}) copy-start(f32[512]{0:T(512)} %param.16) | copy-start | bytes 6148
Sparse Core Ops, SparseCore 0:
  9.2 73.2 all-gather.2
  294.3 69.9 all-gather.4
where the time goes:
time: 393 us; the launch traced here: 392 us
  waiting for transfers between devices  140 us (36%)
  matrix products  139 us (35%)
  blocking collectives  44.2 us (11%)
  other arithmetic  29.1 us (7%)
  local copies, waits for them, and re-layouts  17.8 us (5%)
  between operations  13.5 us (3%)
  loops' own time  8.67 us (2%)
    all_gather x1, waiting for transfers between devices, side_by_side(): out = lax.all_gather(both, axis, axis=dim, tiled=True)  71.8 us
    all_gather x1, waiting for transfers between devices, shards(): piece = lax.all_gather(tail_rows, 'ctx', axis=0, tiled=True)  67.8 us
    dot_general x12, matrix products, attend_block(): jnp.einsum('hgqk,khd->hgqd', weight.astype(jnp.bfloat16), value_block, pr...  57.8 us
    dot_general x12, matrix products, attend_block(): jnp.einsum('qhgd,khd->hgqk', query_heads, key_block, preferred_element_ty...  57.3 us
    all_to_all x1, blocking collectives, sum_at_owner(): tiles = lax.all_to_all(in_blocks(x, dim, size), axis, 0, 0, tiled=True)  44.2 us
    reduce_sum x12, other arithmetic, attend_block(): row_total = row_total * factor + jnp.sum(weight, axis=-1)  18.6 us
    dot_general x1, matrix products, shards(): jnp.einsum('sn,nrc->src', matches, piece, preferred_element_type=jnp.floa...  12.2 us
    another operation x1, loops' own time, shards(): lax.scan(one_step, start_state, (key_split, value_split, jnp.arange(steps...  8.67 us
  transfers between devices with their start and end apart: 2, of which 2 were waited for; matrix products, arithmetic and copies ran while one was open for 1% of the time, Pallas kernels for 0%

commit v1 on v0

v1 whole, which is shorter than its diff:
```python
import functools
import math

import jax
import jax.numpy as jnp
from jax import lax
from jax.experimental import pallas as pl
from jax.experimental.pallas import tpu as pltpu
from jax.sharding import PartitionSpec as P

HEAD_WIDTH = 128
QUERY_PER_KV = 4
GROUP = 4
LOW = -1e30
LOG2_E = 1.4426950408889634


def lookup(table_values, index_values):
    matches = jnp.arange(table_values.shape[0], dtype=jnp.int32)[None, :] == index_values[:, None]
    return jnp.sum(jnp.where(matches, table_values[None, :], 0), axis=1)


def attention_kernel(
    block_rows, holder, own, q_ref, kv_ref, o_ref, qs_ref, m_ref, acc_ref
):
    scale = LOG2_E / math.sqrt(HEAD_WIDTH)
    for s in range(2):
        for h in range(QUERY_PER_KV):
            q = q_ref[
                s * block_rows : (s + 1) * block_rows, h * HEAD_WIDTH : (h + 1) * HEAD_WIDTH
            ].astype(jnp.float32)
            q = q * scale
            high = q.astype(jnp.bfloat16)
            rest = (q - high.astype(jnp.float32)).astype(jnp.bfloat16)
            qs_ref[s, h, :, :HEAD_WIDTH] = high
            qs_ref[s, h, :, HEAD_WIDTH:] = rest
    m_ref[...] = jnp.full_like(m_ref, LOW)
    acc_ref[...] = jnp.zeros_like(acc_ref)
    keys = GROUP * block_rows

    def step(s, group, masked):
        pieces = []
        for j in range(GROUP):
            start = pl.multiple_of(holder[group * GROUP + j] * block_rows, block_rows)
            pieces.append(kv_ref[pl.ds(start, block_rows), :])
        kv = jnp.concatenate(pieces, axis=0)
        k = kv[:, :HEAD_WIDTH]
        k2 = jnp.concatenate([k, k], axis=1)
        v1 = jnp.concatenate([kv[:, HEAD_WIDTH:], jnp.ones_like(k)], axis=1)
        if masked:
            key_at = group * keys + lax.broadcasted_iota(jnp.int32, (block_rows, keys), 1)
            query_at = own[s] * block_rows + lax.broadcasted_iota(
                jnp.int32, (block_rows, keys), 0
            )
            allowed = key_at <= query_at
        for h in range(QUERY_PER_KV):
            scores = lax.dot_general(
                qs_ref[s, h], k2, (((1,), (1,)), ((), ())), preferred_element_type=jnp.float32
            )
            if masked:
                scores = jnp.where(allowed, scores, LOW)
            old = m_ref[s, h]
            newest = jnp.maximum(old, jnp.max(scores, axis=1, keepdims=True))
            weight = jnp.exp2(scores - jnp.concatenate([newest] * (keys // HEAD_WIDTH), axis=1))
            factor = jnp.exp2(old - newest)
            m_ref[s, h] = newest
            acc_ref[s, h] = acc_ref[s, h] * jnp.concatenate([factor, factor], axis=1) + jnp.dot(
                weight.astype(jnp.bfloat16), v1, preferred_element_type=jnp.float32
            )

    for s in range(2):
        last = own[s] // GROUP

        def plain(group, unused):
            step(s, group, False)
            return unused

        lax.fori_loop(0, last, plain, 0)
        step(s, last, True)
    for s in range(2):
        for h in range(QUERY_PER_KV):
            o_ref[
                s * block_rows : (s + 1) * block_rows, h * HEAD_WIDTH : (h + 1) * HEAD_WIDTH
            ] = (acc_ref[s, h, :, :HEAD_WIDTH] / acc_ref[s, h, :, HEAD_WIDTH:]).astype(
                jnp.bfloat16
            )


def attention(holder, own, queries, kv):
    rows = queries.shape[0]
    block_rows = rows // 2
    vmem = pl.BlockSpec(memory_space=pltpu.VMEM)
    return pl.pallas_call(
        functools.partial(attention_kernel, block_rows),
        out_shape=jax.ShapeDtypeStruct(queries.shape, jnp.bfloat16),
        grid_spec=pltpu.PrefetchScalarGridSpec(
            num_scalar_prefetch=2,
            grid=(),
            in_specs=[vmem, vmem],
            out_specs=vmem,
            scratch_shapes=[
                pltpu.VMEM((2, QUERY_PER_KV, block_rows, 2 * HEAD_WIDTH), jnp.bfloat16),
                pltpu.VMEM((2, QUERY_PER_KV, block_rows, HEAD_WIDTH), jnp.float32),
                pltpu.VMEM((2, QUERY_PER_KV, block_rows, 2 * HEAD_WIDTH), jnp.float32),
            ],
        ),
        name="attention",
    )(holder, own, queries, kv)


def inside_kernel(x_ref, taps_ref, o_ref, ext_ref):
    rows = x_ref.shape[1]
    taps = taps_ref.shape[0]
    ext_ref[:taps, :] = jnp.zeros((taps, ext_ref.shape[1]), jnp.float32)
    ext_ref[taps:, :] = x_ref[0].astype(jnp.float32)
    half = rows // 2
    for part in range(2):
        total = jnp.zeros((half, ext_ref.shape[1]), jnp.float32)
        for j in range(8):
            base = 8 + half * part - j
            piece = ext_ref[pl.ds(base, half + taps - 8), :]
            for k in range(taps // 8):
                tap = taps_ref[pl.ds(8 * k + j, 1), :]
                skip = max(0, 8 * k - half * part) // 8 * 8
                if skip >= half:
                    continue
                low = taps - 8 - 8 * k + skip
                term = tap * piece[low : low + half - skip, :]
                if skip:
                    total = jnp.concatenate([total[:skip], total[skip:] + term], axis=0)
                else:
                    total = total + term
        o_ref[0, half * part : half * (part + 1), :] = total


def inside_filter(x, taps):
    blocks, rows, channels = x.shape
    return pl.pallas_call(
        inside_kernel,
        out_shape=jax.ShapeDtypeStruct(x.shape, jnp.float32),
        grid=(blocks, channels // 128),
        in_specs=[
            pl.BlockSpec((1, rows, 128), lambda s, c: (s, 0, c)),
            pl.BlockSpec((taps.shape[0], 128), lambda s, c: (0, c)),
        ],
        out_specs=pl.BlockSpec((1, rows, 128), lambda s, c: (s, 0, c)),
        scratch_shapes=[pltpu.VMEM((rows + taps.shape[0], 128), jnp.float32)],
        name="inside",
    )(x, taps)


def finish_kernel(x_ref, halo_ref, inside_ref, taps_ref, skip_ref, gate_ref, o_ref, ext_ref):
    taps = taps_ref.shape[0]
    ext_ref[:taps, :] = halo_ref[0].astype(jnp.float32)
    ext_ref[taps:, :] = jnp.zeros((taps, ext_ref.shape[1]), jnp.float32)
    half = taps // 2
    added = []
    for part in range(2):
        total = jnp.zeros((half, ext_ref.shape[1]), jnp.float32)
        for j in range(8):
            base = 8 + half * part - j
            piece = ext_ref[pl.ds(base, half + taps - 8), :]
            for k in range(taps // 8):
                tap = taps_ref[pl.ds(8 * k + j, 1), :]
                keep = min(half, 8 * k + 8 - half * part)
                if keep <= 0:
                    continue
                low = taps - 8 - 8 * k
                term = tap * piece[low : low + keep, :]
                if keep < half:
                    total = jnp.concatenate([total[:keep] + term, total[keep:]], axis=0)
                else:
                    total = total + term
        added.append(total)
    rows = x_ref.shape[1]
    added.append(jnp.zeros((rows - taps, ext_ref.shape[1]), jnp.float32))
    filtered = inside_ref[0] + jnp.concatenate(added, axis=0)
    direct = skip_ref[...] * x_ref[0].astype(jnp.float32)
    o_ref[0] = (gate_ref[0].astype(jnp.float32) * (filtered + direct)).astype(jnp.bfloat16)


def finish(x, halo, inside, taps, skip, gate):
    blocks, rows, channels = x.shape
    count = taps.shape[0]
    tile = pl.BlockSpec((1, rows, 128), lambda s, c: (s, 0, c))
    return pl.pallas_call(
        finish_kernel,
        out_shape=jax.ShapeDtypeStruct(x.shape, jnp.bfloat16),
        grid=(blocks, channels // 128),
        in_specs=[
            tile,
            pl.BlockSpec((1, count, 128), lambda s, c: (s, 0, c)),
            tile,
            pl.BlockSpec((count, 128), lambda s, c: (0, c)),
            pl.BlockSpec((1, 128), lambda s, c: (0, c)),
            tile,
        ],
        out_specs=tile,
        scratch_shapes=[pltpu.VMEM((2 * count, 128), jnp.float32)],
        name="finish",
    )(x, halo, inside, taps, skip, gate)


def sum_at_owner(x, axis, dim):
    size = lax.axis_size(axis)
    shape = x.shape
    tiles = x.reshape(*shape[:dim], size, shape[dim] // size, *shape[dim + 1 :])
    tiles = lax.all_to_all(jnp.moveaxis(tiles, dim, 0), axis, 0, 0, tiled=True)
    return jnp.sum(tiles.astype(jnp.float32), axis=0)


def shards(
    block_order,
    queries,
    key_head_matrix,
    value_head_matrix,
    out_weight,
    filter_taps,
    skip_gain,
    gate_values,
):
    local_rows = queries.shape[0]
    block_rows = local_rows // 2
    position = lax.axis_index("ctx")
    own = lookup(block_order, 2 * position + jnp.arange(2, dtype=jnp.int32))
    count = block_order.shape[0]
    places = jnp.arange(count, dtype=jnp.int32)
    holder = jnp.sum(
        jnp.where(block_order[None, :] == places[:, None], places[None, :], 0), axis=1
    )
    kv = lax.all_gather(
        jnp.concatenate([key_head_matrix, value_head_matrix], axis=1), "ctx", axis=0, tiled=True
    )
    attended = attention(holder, own, queries, kv)
    partials = jnp.dot(attended, out_weight, preferred_element_type=jnp.float32)
    projected = sum_at_owner(partials.astype(jnp.bfloat16), "head", 1).astype(jnp.bfloat16)
    channels = projected.shape[1]
    taps = filter_taps.shape[0]
    blocks_here = projected.reshape(2, block_rows, channels)
    tail_rows = blocks_here[:, block_rows - taps :, :]
    piece = lax.all_gather(tail_rows, "ctx", axis=0, tiled=True)
    inside = inside_filter(blocks_here, filter_taps)
    source = lookup(holder, jnp.maximum(own - 1, 0))
    halo = jnp.where((own > 0)[:, None, None], jnp.take(piece, source, axis=0), 0)
    out = finish(
        blocks_here,
        halo,
        inside,
        filter_taps,
        skip_gain[None, :],
        gate_values.reshape(2, block_rows, channels),
    )
    return out.reshape(local_rows, channels)


def solution(mesh):
    return jax.shard_map(
        shards,
        mesh=mesh,
        in_specs=(
            P(),
            P("ctx", "head"),
            P("ctx", "head"),
            P("ctx", "head"),
            P("head", None),
            P(None, "head"),
            P("head"),
            P("ctx", "head"),
        ),
        out_specs=P("ctx", "head"),
        check_vma=False,
    )
```

time: 393 us -> 257 us (0.65)
  matrix products: 139 us -> 4.11 us
  Pallas kernels: 0 us -> 49.2 us
  other arithmetic: 29.1 us -> 5.92 us
  local copies, waits for them, and re-layouts: 17.8 us -> 5.02 us
  loops' own time: 8.67 us -> 0 us
  waiting for transfers between devices: 140 us -> 134 us
    dot_general x25 -> x0, matrix products: 127 us -> none  [the longest x12 57.8 us: attend_block(): jnp.einsum('hgqk,khd->hgqd', weight.astype(jnp.bfloat16), value_block, pr...]
    pallas_call x0 -> x3, Pallas kernels: none -> 49.2 us  [the longest x1 35.5 us: attention(): pl.pallas_call(functools.partial(attention_kernel, block_rows), out_shape...]
    reduce_sum x12 -> x1, other arithmetic: 18.6 us -> 1.26 us  [shards(): jnp.sum(jnp.where(block_order[None, :] == places[:, None], places[None, :...]
    another operation x1 -> x0, loops' own time: 8.67 us -> none  [shards(): lax.scan(one_step, start_state, (key_split, value_split, jnp.arange(steps...]
    conv_general_dilated x1 -> x0, matrix products: 7.51 us -> none  [shards(): lax.conv_general_dilated(extended, kernel, (1,), 'VALID', dimension_numbe...]
    dynamic_slice x12 -> x0, local copies, waits for them, and re-layouts: 7.04 us -> none  [shards(): lax.scan(one_step, start_state, (key_split, value_split, jnp.arange(steps...]
    all_gather x1, waiting for transfers between devices: 67.8 us -> 62.7 us  [shards(): piece = lax.all_gather(tail_rows, 'ctx', axis=0, tiled=True)]
    split x1 -> x0, local copies, waits for them, and re-layouts: 4.74 us -> none  [side_by_side(): jnp.split(out, [sum(widths[:k]) for k in range(1, len(widths))], axis=along)]
  transfers between devices with their start and end apart: 2 -> 2, of which waited for: 2 -> 2; matrix products, arithmetic and copies ran while one was open for 1% -> 1% of each run, Pallas kernels for 0% -> 3%
where the time goes in v1:
time: 257 us; the launch traced here: 256 us
  waiting for transfers between devices  134 us (52%)
  Pallas kernels  49.2 us (19%)
  blocking collectives  44.2 us (17%)
  between operations  13.5 us (5%)
  other arithmetic  5.92 us (2%)
  local copies, waits for them, and re-layouts  5.02 us (2%)
  matrix products  4.11 us (2%)
    all_gather x1, waiting for transfers between devices, shards(): lax.all_gather(jnp.concatenate([key_head_matrix, value_head_matrix], axis...  71.6 us
    all_gather x1, waiting for transfers between devices, shards(): piece = lax.all_gather(tail_rows, 'ctx', axis=0, tiled=True)  62.7 us
    all_to_all x1, blocking collectives, sum_at_owner(): tiles = lax.all_to_all(jnp.moveaxis(tiles, dim, 0), axis, 0, 0, tiled=True)  44.2 us
    pallas_call x1, Pallas kernels, attention(): pl.pallas_call(functools.partial(attention_kernel, block_rows), out_shape...  35.5 us
    pallas_call x1, Pallas kernels, inside_filter(): pl.pallas_call(inside_kernel, out_shape=jax.ShapeDtypeStruct(x.shape, jnp...  7.19 us
    pallas_call x1, Pallas kernels, finish(): pl.pallas_call(finish_kernel, out_shape=jax.ShapeDtypeStruct(x.shape, jnp...  6.55 us
  transfers between devices with their start and end apart: 2, of which 2 were waited for; matrix products, arithmetic and copies ran while one was open for 1% of the time, Pallas kernels for 3%

profile of v1, /device:TPU:1, one launch (start us, length us, event | category | flops | bytes accessed | tf_op | source)
XLA Modules:
  0.0 256.3 jit_solution(14298519574626415724)
XLA Ops:
  6.5 0.0 all-gather.3.cloned.1.call-start
  6.5 1.6 pad_maximum_fusion
  8.2 0.0 all-gather.3.cloned.1.call-update
  8.2 0.0 all-gather.5.cloned.1.call-start
  8.3 1.3 select_reduce_fusion.holder
  9.5 1.4 fusion.own
  10.9 71.6 %all-gather.3.cloned.1.call-done.kv_ref = bf16[12288,256]{1,0:T(8,128)(2,1)} async-done(((bf16[384,256]{1,0:T(8,128)(2,1)}), bf16[12288,256]{1,0:T(8,128)(2,1)}) %all-gather.3.cloned.1.call-update) | async-done | bytes 6291472 | tf_op jit(solution)/shard_map/all_gather | solution.py:231
  82.5 35.5 %attention.1 = bf16[384,512]{1,0:T(8,128)(2,1)} custom-call(s32[64]{0:T(128)} %select_reduce_fusion.holder, s32[2]{0:T(128)} %fusion.own, bf16[384,512]{1,0:T(8,128)(2,1)} %q_ref.1, bf16[12288,256]{1,0:T(8,128)(2,1)} %all-gather.3.cloned.1.call-done.kv_ref), custom_call_target="tpu_custom_call" | custom-call | tf_op jit(solution)/shard_map/attention/pallas_call | solution.py:93
  117.9 4.1 %convolution_convert_fusion = bf16[384,4096]{1,0:T(8,128)(2,1)S(1)} fusion(bf16[384,512]{1,0:T(8,128)(2,1)} %attention.1, bf16[512,4096]{1,0:T(8,128)(2,1)} %param.12), kind=kOutput, calls=%fused_computation.1 | convolution fusion | flops 1612185600 | bytes 7733248 | tf_op jit(solution)/shard_map/dot_general | solution.py:235
  122.1 0.3 copy.13
  122.4 0.0 copy-start.1
  122.4 0.0 copy-start.2
  122.4 44.2 %all_to_all.5 = bf16[8,384,512]{2,1,0:T(8,128)(2,1)S(1)} all-to-all(bf16[8,384,512]{2,1,0:T(8,128)(2,1)S(1)} %bitcast.17), channel_id=1, replica_groups=mesh['ctx'=32,'head'=8] {'head'}, dimensions={0} | all-to-all | bytes 6291456 | tf_op jit(solution)/shard_map/all_to_all | solution.py:208
  166.6 0.7 reduce_sum.43
  167.2 0.0 copy-start
  167.3 0.8 slice.6
  168.0 0.0 all-gather.5.cloned.1.call-update
  168.1 0.0 copy-done.1
  168.1 0.2 fusion.1
  168.3 7.2 %inside.1.inside_ref = f32[2,192,512]{2,1,0:T(8,128)} custom-call(bf16[2,192,512]{2,1,0:T(8,128)(2,1)} %bitcast.19, f32[128,512]{1,0:T(8,128)} %taps_ref.3), custom_call_target="tpu_custom_call" | custom-call | tf_op jit(solution)/shard_map/inside/pallas_call | solution.py:138
  175.5 62.7 %all-gather.5.cloned.1.call-done = bf16[64,128,512]{2,1,0:T(8,128)(2,1)} async-done(((bf16[2,128,512]{2,1,0:T(8,128)(2,1)}), bf16[64,128,512]{2,1,0:T(8,128)(2,1)}) %all-gather.5.cloned.1.call-update) | async-done | bytes 8388624 | tf_op jit(solution)/shard_map/all_gather | solution.py:241
  238.2 3.9 %gather_fusion = bf16[2,128,512]{2,1,0:T(8,128)(2,1)S(1)} fusion(bf16[64,128,512]{2,1,0:T(8,128)(2,1)} %all-gather.5.cloned.1.call-done, s32[1024]{0:T(1024)S(1)} %pad_clamp_fusion), kind=kCustom, calls=%fused_computation | custom fusion | bytes 524296 | tf_op jit(solution)/shard_map/jit(_take)/gather | solution.py:244
  242.1 0.8 select_select_fusion.halo_ref
  242.9 6.5 %finish.1 = bf16[2,192,512]{2,1,0:T(8,128)(2,1)} custom-call(bf16[2,192,512]{2,1,0:T(8,128)(2,1)} %bitcast.20, bf16[2,128,512]{2,1,0:T(8,128)(2,1)} %select_select_fusion.halo_ref, f32[2,192,512]{2,1,0:T(8,128)} %inside.1.inside_ref, f32[128,512]{1,0:T(8,128)} %taps_ref.3, f32[1,512]{1,0:T(1,128)} %bitcast.23, bf16[2,192,512]{2,1,0:T(8,128)(2,1)} %bitcast.22), custom_call_target="tpu_custom_call" | custom-call | tf_op jit(solution)/shard_map/finish/pallas_call | solution.py:186
  (7 shorter events, 0.0 us)
Async XLA Ops:
  6.5 75.9 %all-gather.3.cloned.1.call-start = ((), (), s32[]{:S(2)}) async-start(), calls=%async_computation.1 | async-start | bytes 6488064 | tf_op jit(solution)/shard_map/all_gather | solution.py:231
  8.2 230.0 %all-gather.5.cloned.1.call-start = ((), (), s32[]{:S(2)}) async-start(), calls=%async_computation.2 | async-start | bytes 8650752 | tf_op jit(solution)/shard_map/all_gather | solution.py:241
  122.4 45.7 %copy-start.1 = (s32[2]{0:T(128)S(1)}, s32[2]{0:T(128)}, u32[]{:S(2)}) copy-start(s32[2]{0:T(128)} %fusion.own) | copy-start | bytes 28
  122.4 45.7 %copy-start.2 = (s32[64]{0:T(128)S(1)}, s32[64]{0:T(128)}, u32[]{:S(2)}) copy-start(s32[64]{0:T(128)} %select_reduce_fusion.holder) | copy-start | bytes 772
  167.2 1.1 copy-start
Sparse Core Ops, SparseCore 0:
  9.2 73.2 all-gather.2
  168.2 69.9 all-gather.4
